TPU v7x, 512 devices: a whole 4x8x8 slice. The times are simulated.
512 devices in a mesh: dp: 32 (over y_lo, z), row: 4 (over x), col: 4 (over y_hi, core).
Axes of the slice: x: 4, y: 8 (y_hi: 2, y_lo: 4; y = y_hi * 4 + y_lo), z: 8, core: 2. Of those that a mesh axis runs over, the one named last changes fastest.
Arguments:
- query_out: bfloat16 [6144, 4096], P(('dp', 'row'), 'col'), may hold values from -6 to 6
- query_in: bfloat16 [6144, 4096], P(('dp', 'col')), may hold values from -6 to 6
- out_basis: bfloat16 [4096, 4096], P('col', ('dp', 'row')), may hold values from -0.09375 to 0.09375
- in_basis: bfloat16 [4096, 4096], P(('dp', 'row'), 'col'), may hold values from -0.09375 to 0.09375
- eigvals: float32 [4096, 4096], P(('dp', 'row'), 'col'), may hold values from 16 to 1024
- train_out: bfloat16 [6144, 4096], P(('dp', 'row'), 'col'), may hold values from -0.09375 to 0.09375
- train_in: bfloat16 [6144, 4096], P(('dp', 'col')), may hold values from -0.09375 to 0.09375
Outputs:
- precond: float32 [4096, 4096], P(('dp', 'row'), 'col')
- scores: float32 [6144], P('dp')
All inputs are finite; a program needn't handle non-finite values.
Results may differ from a plain program's by a relative error of at most 0.028.
Values may be sent and summed in bfloat16 or wider, within the bound.
No kernel may reach another device: no remote copies, remote signals or barrier semaphores. Data moves between devices by JAX's collectives and lax.ppermute only.
A program may use at most 64 MiB of HBM per device.

v0:
```python
import jax
import jax.numpy as jnp
from jax import lax
from jax.sharding import PartitionSpec as P

damping = 1.0


def rotate_out(tok_rows, basis_panel):
    gathered = lax.all_gather(tok_rows, "row", axis=0, tiled=True)
    partial_sum = jnp.dot(gathered, basis_panel, preferred_element_type=jnp.float32)
    return lax.psum(partial_sum.astype(jnp.bfloat16), "col")


def rotate_in(tok_rows, basis_panel):
    groups = lax.axis_size("dp")
    row_count = lax.axis_size("row")
    sub_width = tok_rows.shape[1] // (groups * row_count)
    split_rows = tok_rows.reshape(tok_rows.shape[0], groups, row_count, sub_width)
    picked = lax.dynamic_index_in_dim(split_rows, lax.axis_index("row"), 2, keepdims=False)
    picked = picked.reshape(tok_rows.shape[0], groups * sub_width)
    gathered = lax.all_gather(picked, "col", axis=0, tiled=True)
    partial_sum = jnp.dot(gathered, basis_panel, preferred_element_type=jnp.float32)
    return lax.psum(partial_sum.astype(jnp.bfloat16), "row")


def per_device(query_out, query_in, out_basis, in_basis, eigvals, train_out, train_in):
    panel_out = lax.all_gather(out_basis, "dp", axis=1, tiled=True)
    panel_in = lax.all_gather(in_basis, "dp", axis=0, tiled=True)
    query_rot = rotate_out(query_out, panel_out)
    query_inr = rotate_in(query_in, panel_in)
    partial_grad = lax.dot_general(
        query_rot, query_inr, (((0,), (0,)), ((), ())), preferred_element_type=jnp.float32
    )
    rows_own = eigvals.shape[0]
    summed = lax.psum(partial_grad.astype(jnp.bfloat16), "dp").astype(jnp.float32)
    owned = lax.dynamic_slice_in_dim(summed, lax.axis_index("dp") * rows_own, rows_own, 0)
    precond = owned / (eigvals + damping)
    shared = precond.astype(jnp.bfloat16)
    train_rot = rotate_out(train_out, panel_out)
    train_inr = rotate_in(train_in, panel_in)
    mixed = jnp.dot(
        train_rot,
        lax.all_gather(shared, "dp", axis=0, tiled=True),
        preferred_element_type=jnp.float32,
    )
    partial_scores = jnp.sum(mixed * train_inr.astype(jnp.float32), axis=1)
    scores = lax.psum(partial_scores, ("row", "col"))
    return (precond, scores)


def solution(mesh):
    in_specs = (
        P(("dp", "row"), "col"),
        P(("dp", "col"), None),
        P("col", ("dp", "row")),
        P(("dp", "row"), "col"),
        P(("dp", "row"), "col"),
        P(("dp", "row"), "col"),
        P(("dp", "col"), None),
    )
    out_specs = (P(("dp", "row"), "col"), P("dp"))
    return jax.shard_map(
        per_device, mesh=mesh, in_specs=in_specs, out_specs=out_specs, check_vma=False
    )
```

profile of v0, /device:TPU:1, one launch (start us, length us, event | category | flops | bytes accessed | tf_op | source)
XLA Modules:
  0.0 969.9 jit_solution(9535577205798143316)
XLA Ops:
  7.2 0.0 all-gather.6.cloned.1.call-start
  7.2 0.7 all-gather.6.cloned.1.call-update
  7.9 0.0 all-gather.4.cloned.1.call-start
  7.9 0.7 all-gather.4.cloned.1.call-update
  8.6 0.0 all-reduce.10.cloned.1.call-start
  8.7 1.5 copy.9
  10.2 1.5 copy.11
  11.7 0.1 copy.14
  11.8 0.1 copy.13
  12.0 16.7 %all_gather.27 = bf16[192,1024]{1,0:T(8,128)(2,1)S(1)} all-gather(bf16[48,1024]{1,0:T(8,128)(2,1)S(1)} %copy.14), channel_id=1, replica_groups=mesh['dp'=32,'row'=4,'col'=4] {'col'}, dimensions={0}, use_global_device_ids=true | all-gather | bytes 491520 | tf_op jit(solution)/shard_map/all_gather | solution.py:22
  28.7 12.9 %all_gather.23 = bf16[192,1024]{1,0:T(8,128)(2,1)S(1)} all-gather(bf16[48,1024]{1,0:T(8,128)(2,1)S(1)} %copy.13), channel_id=1, replica_groups=mesh['dp'=32,'row'=4,'col'=4] {'col'}, dimensions={0}, use_global_device_ids=true | all-gather | bytes 491520 | tf_op jit(solution)/shard_map/all_gather | solution.py:22
  41.6 106.6 %all-gather.6.cloned.1.call-done = bf16[1024,1024]{1,0:T(8,128)(2,1)} async-done(((bf16[32,1024]{1,0:T(8,128)(2,1)}), bf16[1024,1024]{1,0:T(8,128)(2,1)}) %all-gather.6.cloned.1.call-update) | async-done | bytes 2097168 | tf_op jit(solution)/shard_map/all_gather | solution.py:29
  148.2 0.0 copy-start.1
  148.2 3.1 convolution_convert_fusion.1
  151.3 0.0 copy-done.1
  151.3 0.0 copy-start.3
  151.3 0.0 copy-start.4
  151.3 1.4 convolution_convert_fusion.3
  152.7 0.0 all-reduce.10.cloned.1.call-update
  152.7 0.0 all-reduce.8.cloned.1.call-start
  152.8 0.0 copy-done.3
  152.8 10.9 %all_gather.25 = bf16[192,1024]{1,0:T(8,128)(2,1)S(1)} all-gather(bf16[48,1024]{1,0:T(8,128)(2,1)S(1)} %copy-done.3), channel_id=1, replica_groups=mesh['dp'=32,'row'=4,'col'=4] {'row'}, dimensions={0}, use_global_device_ids=true | all-gather | bytes 491520 | tf_op jit(solution)/shard_map/all_gather | solution.py:10
  163.6 0.0 copy-done.4
  163.6 10.0 %all_gather.21 = bf16[192,1024]{1,0:T(8,128)(2,1)S(1)} all-gather(bf16[48,1024]{1,0:T(8,128)(2,1)S(1)} %copy-done.4), channel_id=1, replica_groups=mesh['dp'=32,'row'=4,'col'=4] {'row'}, dimensions={0}, use_global_device_ids=true | all-gather | bytes 491520 | tf_op jit(solution)/shard_map/all_gather | solution.py:10
  173.6 126.9 %all-gather.4.cloned.1.call-done = bf16[1024,1024]{0,1:T(8,128)(2,1)} async-done(((bf16[1024,32]{0,1:T(8,128)(2,1)}), bf16[1024,1024]{0,1:T(8,128)(2,1)}) %all-gather.4.cloned.1.call-update) | async-done | bytes 2097168 | tf_op jit(solution)/shard_map/all_gather | solution.py:28
  300.6 0.0 copy-start
  300.6 3.3 convolution_convert_fusion.2
  303.9 0.0 copy-done
  303.9 1.6 convolution_convert_fusion.4
  305.5 0.0 all-reduce.8.cloned.1.call-update
  305.5 0.0 all-reduce.6.cloned.1.call-start
  305.6 68.1 %all-reduce.10.cloned.1.call-done = (bf16[192,1024]{1,0:T(8,128)(2,1)}, bf16[192,1024]{1,0:T(8,128)(2,1)}) async-done(((bf16[192,1024]{1,0:T(8,128)(2,1)}, bf16[192,1024]{1,0:T(8,128)(2,1)}), (bf16[192,1024]{1,0:T(8,128)(2,1)}, bf16[192,1024]{1,0:T(8,128)(2,1)})) %all-reduce.10.cloned.1.call-update) | async-done | bytes 786448 | tf_op jit(solution)/shard_map/psum | solution.py:24
  373.7 75.0 %all-reduce.8.cloned.1.call-done = (bf16[192,1024]{1,0:T(8,128)(2,1)}, bf16[192,1024]{1,0:T(8,128)(2,1)}) async-done(((bf16[192,1024]{1,0:T(8,128)(2,1)}, bf16[192,1024]{1,0:T(8,128)(2,1)}), (bf16[192,1024]{1,0:T(8,128)(2,1)}, bf16[192,1024]{1,0:T(8,128)(2,1)})) %all-reduce.8.cloned.1.call-update) | async-done | bytes 786448 | tf_op jit(solution)/shard_map/psum | solution.py:12
  448.7 0.0 copy-start.2
  448.7 0.0 copy-start.5
  448.7 0.0 copy-start.6
  448.7 3.3 convolution_convert_fusion
  451.9 0.0 all-reduce.6.cloned.1.call-update
  452.0 0.0 all-gather.8.cloned.1.call-start
  452.0 290.8 %all-reduce.6.cloned.1.call-done = bf16[1024,1024]{1,0:T(8,128)(2,1)} async-done(((bf16[1024,1024]{1,0:T(8,128)(2,1)}), bf16[1024,1024]{1,0:T(8,128)(2,1)}) %all-reduce.6.cloned.1.call-update) | async-done | bytes 2097168 | tf_op jit(solution)/shard_map/psum | solution.py:36
  742.8 0.0 copy-done.2
  742.8 1.5 fusion.1
  744.3 0.0 all-gather.8.cloned.1.call-update
  744.4 150.6 %all-gather.8.cloned.1.call-done = bf16[1024,1024]{1,0:T(8,128)(2,1)} async-done(((bf16[32,1024]{1,0:T(8,128)(2,1)}), bf16[1024,1024]{1,0:T(8,128)(2,1)}) %all-gather.8.cloned.1.call-update) | async-done | bytes 2097168 | tf_op jit(solution)/shard_map/all_gather | solution.py:44
  895.0 0.0 copy-done.5
  895.0 0.0 copy-done.6
  895.0 2.3 fusion
  897.2 65.8 %psum.47 = f32[192]{0:T(256)} all-reduce(f32[192]{0:T(256)S(1)} %fusion), channel_id=1, replica_groups=mesh['dp'=32,'row'=4,'col'=4] {'row','col'}, use_global_device_ids=true, to_apply=%region_6.7 | all-reduce | flops 192 | bytes 1536 | tf_op jit(solution)/shard_map/psum | solution.py:48
  (1 shorter events, 0.0 us)
Async XLA Ops:
  7.2 141.1 %all-gather.6.cloned.1.call-start = ((), (), s32[]{:S(2)}) async-start(), calls=%async_computation.1 | async-start | bytes 2162688 | tf_op jit(solution)/shard_map/all_gather | solution.py:29
  7.9 292.7 %all-gather.4.cloned.1.call-start = ((), (), s32[]{:S(2)}) async-start(), calls=%async_computation | async-start | bytes 2162688 | tf_op jit(solution)/shard_map/all_gather | solution.py:28
  8.6 365.1 %all-reduce.10.cloned.1.call-start = ((), (), s32[]{:S(2)}) async-start(), calls=%async_computation.5 | async-start | bytes 1572864 | tf_op jit(solution)/shard_map/psum | solution.py:24
  148.2 3.1 copy-start.1
  151.3 1.4 copy-start.3
  151.3 12.3 %copy-start.4 = (bf16[48,1024]{1,0:T(8,128)(2,1)S(1)}, bf16[48,1024]{1,0:T(8,128)(2,1)}, u32[]{:S(2)}) copy-start(bf16[48,1024]{1,0:T(8,128)(2,1)} %param.7) | copy-start | bytes 294916
  152.7 295.9 %all-reduce.8.cloned.1.call-start = ((), (), s32[]{:S(2)}) async-start(), calls=%async_computation.4 | async-start | bytes 1572864 | tf_op jit(solution)/shard_map/psum | solution.py:12
  300.6 3.3 copy-start
  305.5 437.3 %all-reduce.6.cloned.1.call-start = ((), (), s32[]{:S(2)}) async-start(), calls=%async_computation.2 | async-start | bytes 4194304 | tf_op jit(solution)/shard_map/psum | solution.py:36
  448.7 294.2 %copy-start.2 = (f32[32,1024]{1,0:T(8,128)S(1)}, f32[32,1024]{1,0:T(8,128)}, u32[]{:S(2)}) copy-start(f32[32,1024]{1,0:T(8,128)} %param.11) | copy-start | bytes 393220
  448.7 446.3 %copy-start.5 = (bf16[192,1024]{1,0:T(8,128)(2,1)S(1)}, bf16[192,1024]{1,0:T(8,128)(2,1)}, u32[]{:S(2)}) copy-start(bf16[192,1024]{1,0:T(8,128)(2,1)} %get-tuple-element.5) | copy-start | bytes 1179652
  448.7 446.3 %copy-start.6 = (bf16[192,1024]{1,0:T(8,128)(2,1)S(1)}, bf16[192,1024]{1,0:T(8,128)(2,1)}, u32[]{:S(2)}) copy-start(bf16[192,1024]{1,0:T(8,128)(2,1)} %get-tuple-element.3) | copy-start | bytes 1179652
  452.0 443.0 %all-gather.8.cloned.1.call-start = ((), (), s32[]{:S(2)}) async-start(), calls=%async_computation.3 | async-start | bytes 2162688 | tf_op jit(solution)/shard_map/all_gather | solution.py:44
Sparse Core Ops, SparseCore 0:
  10.0 138.1 all-gather.5
  150.3 150.2 all-gather.3
  303.0 70.6 all-reduce.9
  376.6 72.0 all-reduce.7
  452.1 290.6 all-reduce.5
  744.7 150.1 all-gather.7
where the time goes:
time: 970 us
  waiting for transfers between devices  819 us (84%)
  blocking collectives  116 us (12%)
  matrix products  14.9 us (2%)
  between operations  14.2 us (1%)
    psum x1, waiting for transfers between devices, per_device(): lax.psum(partial_grad.astype(jnp.bfloat16), 'dp').astype(jnp.float32)  291 us
    all_gather x1, waiting for transfers between devices, per_device(): lax.all_gather(shared, 'dp', axis=0, tiled=True)  151 us
    all_gather x1, waiting for transfers between devices, per_device(): panel_out = lax.all_gather(out_basis, 'dp', axis=1, tiled=True)  127 us
    all_gather x1, waiting for transfers between devices, per_device(): panel_in = lax.all_gather(in_basis, 'dp', axis=0, tiled=True)  107 us
    psum x1, waiting for transfers between devices, rotate_out(): return lax.psum(partial_sum.astype(jnp.bfloat16), 'col')  75 us
    psum x1, waiting for transfers between devices, rotate_in(): return lax.psum(partial_sum.astype(jnp.bfloat16), 'row')  68.1 us
    psum x1, blocking collectives, per_device(): scores = lax.psum(partial_scores, ('row', 'col'))  65.8 us
    all_gather x2, blocking collectives, rotate_in(): gathered = lax.all_gather(picked, 'col', axis=0, tiled=True)  29.6 us
  transfers between devices with their start and end apart: 6, of which 6 were waited for; matrix products, arithmetic and copies ran while one was open for 1% of the time, Pallas kernels for 0%

commit v1 on v0

--- a/solution.py
+++ b/solution.py
@@ -2,6 +2,7 @@
 import jax.numpy as jnp
 from jax import lax
 from jax.sharding import PartitionSpec as P
+from jax.lax import all_to_all, axis_size
 
 damping = 1.0
 
@@ -39,11 +40,13 @@
     shared = precond.astype(jnp.bfloat16)
     train_rot = rotate_out(train_out, panel_out)
     train_inr = rotate_in(train_in, panel_in)
-    mixed = jnp.dot(
-        train_rot,
-        lax.all_gather(shared, "dp", axis=0, tiled=True),
-        preferred_element_type=jnp.float32,
-    )
+
+    def classes_deliver(arr_in, which_dim, peer_axis):
+        finding = jnp.stack([arr_in for _ in range(axis_size(peer_axis))], axis=0)
+        plain = all_to_all(finding, peer_axis, 0, 0)
+        return jnp.concatenate(plain, axis=which_dim)
+
+    mixed = jnp.dot(train_rot, classes_deliver(shared, 0, "dp"), preferred_element_type=jnp.float32)
     partial_scores = jnp.sum(mixed * train_inr.astype(jnp.float32), axis=1)
     scores = lax.psum(partial_scores, ("row", "col"))
     return (precond, scores)

time: 970 us -> 863 us (0.89)
  waiting for transfers between devices: 819 us -> 654 us
  blocking collectives: 116 us -> 177 us
    all_gather x1 -> x0, waiting for transfers between devices: 151 us -> none  [per_device(): lax.all_gather(shared, 'dp', axis=0, tiled=True)]
    all_to_all x0 -> x1, blocking collectives: none -> 33.7 us  [classes_deliver(): plain = all_to_all(finding, peer_axis, 0, 0)]
    all_gather x2, blocking collectives: 29.6 us -> 44.7 us  [rotate_in(): gathered = lax.all_gather(picked, 'col', axis=0, tiled=True)]
    psum x1, waiting for transfers between devices: 68.1 us -> 53.7 us  [rotate_in(): return lax.psum(partial_sum.astype(jnp.bfloat16), 'row')]
    psum x1, blocking collectives: 65.8 us -> 77.7 us  [per_device(): scores = lax.psum(partial_scores, ('row', 'col'))]
    all_gather x1, waiting for transfers between devices: 127 us -> 116 us  [per_device(): panel_out = lax.all_gather(out_basis, 'dp', axis=1, tiled=True)]
    psum x1, waiting for transfers between devices: 75 us -> 85.3 us  [rotate_out(): return lax.psum(partial_sum.astype(jnp.bfloat16), 'col')]
  transfers between devices with their start and end apart: 6 -> 5, of which waited for: 6 -> 5; matrix products, arithmetic and copies ran while one was open for 1% -> 1% of each run, Pallas kernels for 0% -> 0%
where the time goes in v1:
time: 863 us
  waiting for transfers between devices  654 us (76%)
  blocking collectives  177 us (21%)
  between operations  13.9 us (2%)
  matrix products  13.3 us (2%)
    psum x1, waiting for transfers between devices, per_device(): lax.psum(partial_grad.astype(jnp.bfloat16), 'dp').astype(jnp.float32)  295 us
    all_gather x1, waiting for transfers between devices, per_device(): panel_out = lax.all_gather(out_basis, 'dp', axis=1, tiled=True)  116 us
    all_gather x1, waiting for transfers between devices, per_device(): panel_in = lax.all_gather(in_basis, 'dp', axis=0, tiled=True)  102 us
    psum x1, waiting for transfers between devices, rotate_out(): return lax.psum(partial_sum.astype(jnp.bfloat16), 'col')  85.3 us
    psum x1, blocking collectives, per_device(): scores = lax.psum(partial_scores, ('row', 'col'))  77.7 us
    psum x1, waiting for transfers between devices, rotate_in(): return lax.psum(partial_sum.astype(jnp.bfloat16), 'row')  53.7 us
    all_gather x2, blocking collectives, rotate_in(): gathered = lax.all_gather(picked, 'col', axis=0, tiled=True)  44.7 us
    all_to_all x1, blocking collectives, classes_deliver(): plain = all_to_all(finding, peer_axis, 0, 0)  33.7 us
  transfers between devices with their start and end apart: 5, of which 5 were waited for; matrix products, arithmetic and copies ran while one was open for 1% of the time, Pallas kernels for 0%

profile of v1, /device:TPU:1, one launch (start us, length us, event | category | flops | bytes accessed | tf_op | source)
XLA Modules:
  0.0 863.0 jit_solution(17560882267786839714)
XLA Ops:
  7.2 0.0 all-gather.3.cloned.1.call-start
  7.2 0.7 all-gather.3.cloned.1.call-update
  7.9 0.0 all-gather.5.cloned.1.call-start
  7.9 0.7 all-gather.5.cloned.1.call-update
  8.6 0.0 all-reduce.8.cloned.1.call-start
  8.7 0.0 copy-start.3
  8.7 0.0 copy-start.4
  8.7 1.5 copy.11
  10.2 1.5 copy.9
  11.8 0.1 copy.13
  11.9 0.0 copy-done.3
  11.9 10.8 %all_gather.18 = bf16[192,1024]{1,0:T(8,128)(2,1)S(1)} all-gather(bf16[48,1024]{1,0:T(8,128)(2,1)S(1)} %copy-done.3), channel_id=1, replica_groups=mesh['dp'=32,'row'=4,'col'=4] {'row'}, dimensions={0}, use_global_device_ids=true | all-gather | bytes 491520 | tf_op jit(solution)/shard_map/all_gather | solution.py:11
  22.7 0.0 copy-done.4
  22.7 9.6 %all_gather.22 = bf16[192,1024]{1,0:T(8,128)(2,1)S(1)} all-gather(bf16[48,1024]{1,0:T(8,128)(2,1)S(1)} %copy-done.4), channel_id=1, replica_groups=mesh['dp'=32,'row'=4,'col'=4] {'row'}, dimensions={0}, use_global_device_ids=true | all-gather | bytes 491520 | tf_op jit(solution)/shard_map/all_gather | solution.py:11
  32.3 115.9 %all-gather.3.cloned.1.call-done = bf16[1024,1024]{0,1:T(8,128)(2,1)} async-done(((bf16[1024,32]{0,1:T(8,128)(2,1)}), bf16[1024,1024]{0,1:T(8,128)(2,1)}) %all-gather.3.cloned.1.call-update) | async-done | bytes 2097168 | tf_op jit(solution)/shard_map/all_gather | solution.py:29
  148.3 0.0 copy-start.1
  148.3 3.3 convolution_convert_fusion.4
  151.6 0.0 copy-done.1
  151.6 1.6 convolution_convert_fusion.2
  153.2 0.0 all-reduce.8.cloned.1.call-update
  153.2 0.0 all-reduce.10.cloned.1.call-start
  153.3 33.9 %all_gather.20 = bf16[192,1024]{1,0:T(8,128)(2,1)S(1)} all-gather(bf16[48,1024]{1,0:T(8,128)(2,1)S(1)} %copy.13), channel_id=1, replica_groups=mesh['dp'=32,'row'=4,'col'=4] {'col'}, dimensions={0}, use_global_device_ids=true | all-gather | bytes 491520 | tf_op jit(solution)/shard_map/all_gather | solution.py:23
  187.2 0.1 copy.14
  187.3 10.8 %all_gather.23 = bf16[192,1024]{1,0:T(8,128)(2,1)S(1)} all-gather(bf16[48,1024]{1,0:T(8,128)(2,1)S(1)} %copy.14), channel_id=1, replica_groups=mesh['dp'=32,'row'=4,'col'=4] {'col'}, dimensions={0}, use_global_device_ids=true | all-gather | bytes 491520 | tf_op jit(solution)/shard_map/all_gather | solution.py:23
  198.1 102.2 %all-gather.5.cloned.1.call-done = bf16[1024,1024]{1,0:T(8,128)(2,1)} async-done(((bf16[32,1024]{1,0:T(8,128)(2,1)}), bf16[1024,1024]{1,0:T(8,128)(2,1)}) %all-gather.5.cloned.1.call-update) | async-done | bytes 2097168 | tf_op jit(solution)/shard_map/all_gather | solution.py:30
  300.4 0.0 copy-start
  300.4 3.1 convolution_convert_fusion.3
  303.4 0.0 copy-done
  303.4 1.3 convolution_convert_fusion.1
  304.8 0.0 all-reduce.10.cloned.1.call-update
  304.8 0.0 all-reduce.6.cloned.1.call-start
  304.9 85.3 %all-reduce.8.cloned.1.call-done = (bf16[192,1024]{1,0:T(8,128)(2,1)}, bf16[192,1024]{1,0:T(8,128)(2,1)}) async-done(((bf16[192,1024]{1,0:T(8,128)(2,1)}, bf16[192,1024]{1,0:T(8,128)(2,1)}), (bf16[192,1024]{1,0:T(8,128)(2,1)}, bf16[192,1024]{1,0:T(8,128)(2,1)})) %all-reduce.8.cloned.1.call-update) | async-done | bytes 786448 | tf_op jit(solution)/shard_map/psum | solution.py:13
  390.2 53.7 %all-reduce.10.cloned.1.call-done = (bf16[192,1024]{1,0:T(8,128)(2,1)}, bf16[192,1024]{1,0:T(8,128)(2,1)}) async-done(((bf16[192,1024]{1,0:T(8,128)(2,1)}, bf16[192,1024]{1,0:T(8,128)(2,1)}), (bf16[192,1024]{1,0:T(8,128)(2,1)}, bf16[192,1024]{1,0:T(8,128)(2,1)})) %all-reduce.10.cloned.1.call-update) | async-done | bytes 786448 | tf_op jit(solution)/shard_map/psum | solution.py:25
  443.9 0.0 copy-start.2
  443.9 3.2 convolution_convert_fusion
  447.2 0.0 all-reduce.6.cloned.1.call-update
  447.2 295.3 %all-reduce.6.cloned.1.call-done = bf16[1024,1024]{1,0:T(8,128)(2,1)} async-done(((bf16[1024,1024]{1,0:T(8,128)(2,1)}), bf16[1024,1024]{1,0:T(8,128)(2,1)}) %all-reduce.6.cloned.1.call-update) | async-done | bytes 2097168 | tf_op jit(solution)/shard_map/psum | solution.py:37
  742.5 0.0 copy-done.2
  742.5 1.5 fusion.1
  744.0 0.2 stack.2
  744.3 0.0 copy-start.5
  744.3 0.0 copy-start.6
  744.3 33.7 %all_to_all.5 = bf16[32,32,1024]{2,1,0:T(8,128)(2,1)S(1)} all-to-all(bf16[32,32,1024]{2,1,0:T(8,128)(2,1)S(1)} %stack.2), channel_id=1, replica_groups=mesh['dp'=32,'row'=4,'col'=4] {'dp'}, dimensions={0} | all-to-all | bytes 4194304 | tf_op jit(solution)/shard_map/all_to_all | solution.py:46
  778.1 0.0 copy-done.5
  778.1 0.0 copy-done.6
  778.1 0.7 fusion
  778.7 77.7 %psum.47 = f32[192]{0:T(256)} all-reduce(f32[192]{0:T(256)S(1)} %fusion), channel_id=1, replica_groups=mesh['dp'=32,'row'=4,'col'=4] {'row','col'}, use_global_device_ids=true, to_apply=%region_6.7 | all-reduce | flops 192 | bytes 1536 | tf_op jit(solution)/shard_map/psum | solution.py:51
  (1 shorter events, 0.0 us)
Async XLA Ops:
  7.2 141.1 %all-gather.3.cloned.1.call-start = ((), (), s32[]{:S(2)}) async-start(), calls=%async_computation.1 | async-start | bytes 2162688 | tf_op jit(solution)/shard_map/all_gather | solution.py:29
  7.9 292.5 %all-gather.5.cloned.1.call-start = ((), (), s32[]{:S(2)}) async-start(), calls=%async_computation.2 | async-start | bytes 2162688 | tf_op jit(solution)/shard_map/all_gather | solution.py:30
  8.6 381.6 %all-reduce.8.cloned.1.call-start = ((), (), s32[]{:S(2)}) async-start(), calls=%async_computation.4 | async-start | bytes 1572864 | tf_op jit(solution)/shard_map/psum | solution.py:13
  8.7 3.2 copy-start.3
  8.7 14.0 %copy-start.4 = (bf16[48,1024]{1,0:T(8,128)(2,1)S(1)}, bf16[48,1024]{1,0:T(8,128)(2,1)}, u32[]{:S(2)}) copy-start(bf16[48,1024]{1,0:T(8,128)(2,1)} %param.12) | copy-start | bytes 294916
  148.3 3.3 copy-start.1
  153.2 290.7 %all-reduce.10.cloned.1.call-start = ((), (), s32[]{:S(2)}) async-start(), calls=%async_computation.5 | async-start | bytes 1572864 | tf_op jit(solution)/shard_map/psum | solution.py:25
  300.4 3.1 copy-start
  304.8 437.7 %all-reduce.6.cloned.1.call-start = ((), (), s32[]{:S(2)}) async-start(), calls=%async_computation.3 | async-start | bytes 4194304 | tf_op jit(solution)/shard_map/psum | solution.py:37
  443.9 298.6 %copy-start.2 = (f32[32,1024]{1,0:T(8,128)S(1)}, f32[32,1024]{1,0:T(8,128)}, u32[]{:S(2)}) copy-start(f32[32,1024]{1,0:T(8,128)} %param.11) | copy-start | bytes 393220
  744.3 33.8 %copy-start.5 = (bf16[192,1024]{1,0:T(8,128)(2,1)S(1)}, bf16[192,1024]{1,0:T(8,128)(2,1)}, u32[]{:S(2)}) copy-start(bf16[192,1024]{1,0:T(8,128)(2,1)} %get-tuple-element.3) | copy-start | bytes 1179652
  744.3 33.8 %copy-start.6 = (bf16[192,1024]{1,0:T(8,128)(2,1)S(1)}, bf16[192,1024]{1,0:T(8,128)(2,1)}, u32[]{:S(2)}) copy-start(bf16[192,1024]{1,0:T(8,128)(2,1)} %get-tuple-element.5) | copy-start | bytes 1179652
Sparse Core Ops, SparseCore 0:
  10.1 138.1 all-gather.2
  150.3 149.9 all-gather.4
  303.4 86.7 all-reduce.7
  392.4 51.4 all-reduce.9
  447.3 295.1 all-reduce.5
